TPU v7x, 256 devices: a whole 4x4x8 slice. The times are simulated.
256 devices in a mesh: row: 16 (over z, x_lo), col: 16 (over y, x_hi, core).
Axes of the slice: x: 4 (x_hi: 2, x_lo: 2; x = x_hi * 2 + x_lo), y: 4, z: 8, core: 2. Of those that a mesh axis runs over, the one named last changes fastest.
Arguments:
- fock_matrix: bfloat16 [12288, 12288], P('row', 'col'), as said below
- density: bfloat16 [12288, 12288], P('row', 'col'), as said below
- intersection: bfloat16 [12288, 12288], P('row', 'col'), as said below
- pattern: int32 [96, 96], replicated, may hold values from 0 to 1, as said below
Outputs:
- gradient_panel: bfloat16 [12288, 2048], P('row', 'col')
Inputs may be any that keep to these rules, and one draw needn't show every extreme that they name: `pattern`: symmetric, with ones on the diagonal; pattern[i, j] is 1 exactly where the centres of blocks i and j lie within the neighbour cutoff of each other. `fock_matrix`: symmetric; zero in every block (i, j) with pattern[i, j] == 0. `density`: symmetric; zero in every block (i, j) with pattern[i, j] == 0. `intersection`: symmetric; zero in every block (i, j) with pattern[i, j] == 0.
All inputs are finite; a program needn't handle non-finite values.
Results may differ from a plain program's by a relative error of at most 0.023.
Values may be sent and summed in bfloat16 or wider, within the bound.
A program may use at most 128 MiB of HBM per device.

v0:
```python
import jax
import jax.numpy as jnp
from jax import lax
from jax.sharding import PartitionSpec as P

BLK = 128


def local(fock_matrix, density, intersection, pattern):
    col_index = lax.axis_index("col")
    tile_rows, tile_cols = fock_matrix.shape
    blocks_col = tile_cols // BLK
    panel_local = jnp.stack([intersection[:, :BLK], fock_matrix[:, :BLK]])
    row_partials = jnp.einsum(
        "ki,skp->sip",
        density,
        lax.all_gather(panel_local, "col", axis=2, tiled=True),
        preferred_element_type=jnp.float32,
    )
    panel_width = row_partials.shape[2]
    owned_blocks = lax.dynamic_slice_in_dim(pattern, col_index * blocks_col, blocks_col, 0)[
        :, ::blocks_col
    ]
    keep_mask = jnp.broadcast_to(
        owned_blocks.astype(jnp.float32)[:, None, :, None],
        (blocks_col, BLK, owned_blocks.shape[1], BLK),
    ).reshape(tile_cols, panel_width)
    combined = lax.psum(row_partials.astype(jnp.bfloat16), "row").astype(jnp.float32)
    filtered = (combined * keep_mask[None]).astype(jnp.bfloat16)
    column_term = jnp.dot(fock_matrix, filtered[0], preferred_element_type=jnp.float32)
    column_term = column_term - jnp.dot(
        intersection, filtered[1], preferred_element_type=jnp.float32
    )
    return lax.psum_scatter(
        column_term.astype(jnp.bfloat16), "col", scatter_dimension=1, tiled=True
    )


def solution(mesh):
    return jax.shard_map(
        local,
        mesh=mesh,
        in_specs=(P("row", "col"), P("row", "col"), P("row", "col"), P()),
        out_specs=P("row", "col"),
        check_vma=False,
    )
```

profile of v0, /device:TPU:1, one launch (start us, length us, event | category | flops | bytes accessed | tf_op | source)
XLA Modules:
  0.0 481.8 jit_solution(13129948686597280517)
XLA Ops:
  6.5 0.0 copy-start
  6.5 0.0 all-gather.2.cloned.1.call-start
  6.5 1.0 slice.16
  7.6 0.1 copy.14
  7.7 0.9 slice.15
  8.7 0.1 copy.13
  8.8 0.8 pad_maximum_fusion
  9.6 0.0 all-gather.2.cloned.1.call-update
  9.6 0.0 all-reduce.2.cloned.1.call-start
  9.7 73.9 %all-gather.2.cloned.1.call-done = bf16[2,768,2048]{1,2,0:T(8,128)(2,1)} async-done(((bf16[2,768,128]{1,2,0:T(8,128)(2,1)}), bf16[2,768,2048]{1,2,0:T(8,128)(2,1)}) %all-gather.2.cloned.1.call-update) | async-done | bytes 6291472 | tf_op jit(solution)/shard_map/all_gather | solution.py:17
  83.6 0.0 copy-done
  83.6 9.7 %convert_bitcast_fusion = bf16[2,768,2048]{1,2,0:T(8,128)(2,1)} fusion(bf16[2,768,2048]{1,2,0:T(8,128)(2,1)} %all-gather.2.cloned.1.call-done, bf16[768,768]{1,0:T(8,128)(2,1)S(1)} %copy-done), kind=kOutput, calls=%fused_computation.3 | convolution fusion | flops 4834983936 | bytes 13762560 | tf_op jit(solution)/shard_map/ki,skp->sip/dot_general | solution.py:14
  93.3 0.0 all-reduce.2.cloned.1.call-update
  93.3 0.0 reduce-scatter.2.cloned.1.call-start
  93.4 0.7 constant_dynamic-slice_fusion
  94.1 0.1 slice.17
  94.2 0.5 broadcast_in_dim.2
  94.7 5.6 %copy.17 = f32[96,8,16,128]{3,1,2,0:T(8,128)} copy(f32[96,8,16,128]{3,2,1,0:T(8,128)S(1)} %bitcast.25) | data formatting | bytes 12582912
  100.3 6.6 %copy.11 = f32[768,2048]{0,1:T(8,128)} copy(f32[768,2048]{1,0:T(8,128)} %bitcast.26) | data formatting | bytes 12582912 | tf_op jit(solution)/shard_map/mul | solution.py:29
  106.9 0.0 copy-start.2
  106.9 266.3 %all-reduce.2.cloned.1.call-done = bf16[2,768,2048]{1,2,0:T(8,128)(2,1)} async-done(((bf16[2,768,2048]{1,2,0:T(8,128)(2,1)}), bf16[2,768,2048]{1,2,0:T(8,128)(2,1)}) %all-reduce.2.cloned.1.call-update) | async-done | bytes 6291472 | tf_op jit(solution)/shard_map/psum | solution.py:28
  373.2 8.4 %multiply_convert_fusion = bf16[2,768,2048]{1,2,0:T(8,128)(2,1)} fusion(bf16[2,768,2048]{1,2,0:T(8,128)(2,1)} %all-reduce.2.cloned.1.call-done, f32[768,2048]{0,1:T(8,128)} %copy.11), kind=kLoop, calls=%fused_computation | loop fusion | flops 9437184 | bytes 18874368 | tf_op jit(solution)/shard_map/convert_element_type | solution.py:29
  381.6 0.0 copy-done.2
  381.6 0.0 copy-start.1
  381.6 0.0 copy-start.3
  381.6 4.7 fusion
  386.4 0.0 copy-done.1
  386.4 0.0 copy-done.3
  386.4 4.1 fusion.1
  390.4 0.0 reduce-scatter.2.cloned.1.call-update
  390.5 83.1 %reduce-scatter.2.cloned.1.call-done = bf16[768,128]{0,1:T(8,128)(2,1)} async-done(((bf16[768,2048]{0,1:T(8,128)(2,1)}), bf16[768,128]{0,1:T(8,128)(2,1)}) %reduce-scatter.2.cloned.1.call-update) | async-done | bytes 196624 | tf_op jit(solution)/shard_map/reduce_scatter | solution.py:34
  473.5 1.7 copy.12
  (1 shorter events, 0.0 us)
Async XLA Ops:
  6.5 77.0 %copy-start = (bf16[768,768]{1,0:T(8,128)(2,1)S(1)}, bf16[768,768]{1,0:T(8,128)(2,1)}, u32[]{:S(2)}) copy-start(bf16[768,768]{1,0:T(8,128)(2,1)} %param.5) | copy-start | bytes 3538948
  6.5 77.0 %all-gather.2.cloned.1.call-start = ((), (), s32[]{:S(2)}) async-start(), calls=%async_computation.1 | async-start | bytes 6684672 | tf_op jit(solution)/shard_map/all_gather | solution.py:17
  9.6 363.6 %all-reduce.2.cloned.1.call-start = ((), (), s32[]{:S(2)}) async-start(), calls=%async_computation.2 | async-start | bytes 12582912 | tf_op jit(solution)/shard_map/psum | solution.py:28
  93.3 380.2 %reduce-scatter.2.cloned.1.call-start = ((), (), s32[]{:S(2)}) async-start(), calls=%async_computation.3 | async-start | bytes 3342336 | tf_op jit(solution)/shard_map/reduce_scatter | solution.py:34
  106.9 274.7 %copy-start.2 = (bf16[768,768]{1,0:T(8,128)(2,1)S(1)}, bf16[768,768]{1,0:T(8,128)(2,1)}, u32[]{:S(2)}) copy-start(bf16[768,768]{1,0:T(8,128)(2,1)} %param.4) | copy-start | bytes 3538948
  381.6 4.8 copy-start.1
  381.6 4.8 copy-start.3
Sparse Core Ops, SparseCore 0:
  10.2 73.3 all-gather.1
  93.4 279.7 all-reduce.1
  390.6 82.8 reduce-scatter.1
where the time goes:
time: 482 us
  waiting for transfers between devices  423 us (88%)
  matrix products  18.6 us (4%)
  local copies, waits for them, and re-layouts  17.5 us (4%)
  between operations  13.2 us (3%)
  other arithmetic  9.15 us (2%)
    psum x1, waiting for transfers between devices, local(): lax.psum(row_partials.astype(jnp.bfloat16), 'row').astype(jnp.float32)  266 us
    reduce_scatter x1, waiting for transfers between devices, local(): lax.psum_scatter(column_term.astype(jnp.bfloat16), 'col', scatter_dimensi...  83.1 us
    all_gather x1, waiting for transfers between devices, local(): lax.all_gather(panel_local, 'col', axis=2, tiled=True)  73.9 us
    dot_general x1, matrix products, local(): jnp.einsum('ki,skp->sip', density, lax.all_gather(panel_local, 'col', axi...  9.74 us
  transfers between devices with their start and end apart: 3, of which 3 were waited for; matrix products, arithmetic and copies ran while one was open for 3% of the time, Pallas kernels for 0%

commit v1 on v0

--- a/solution.py
+++ b/solution.py
@@ -25,7 +25,9 @@
         owned_blocks.astype(jnp.float32)[:, None, :, None],
         (blocks_col, BLK, owned_blocks.shape[1], BLK),
     ).reshape(tile_cols, panel_width)
-    combined = lax.psum(row_partials.astype(jnp.bfloat16), "row").astype(jnp.float32)
+    combined = jnp.sum(lax.all_gather(row_partials.astype(jnp.bfloat16), "row"), axis=0).astype(
+        jnp.float32
+    )
     filtered = (combined * keep_mask[None]).astype(jnp.bfloat16)
     column_term = jnp.dot(fock_matrix, filtered[0], preferred_element_type=jnp.float32)
     column_term = column_term - jnp.dot(

time: 482 us -> 2290 us (4.75)
  waiting for transfers between devices: 423 us -> 2180 us
  other arithmetic: 9.15 us -> 44 us
    all_gather x0 -> x1, waiting for transfers between devices: none -> 2020 us  [local(): lax.all_gather(row_partials.astype(jnp.bfloat16), 'row')]
    psum x1 -> x0, waiting for transfers between devices: 266 us -> none  [local(): lax.psum(row_partials.astype(jnp.bfloat16), 'row').astype(jnp.float32)]
    reduce_sum x0 -> x1, other arithmetic: none -> 34.7 us  [local(): jnp.sum(lax.all_gather(row_partials.astype(jnp.bfloat16), 'row'), axis=0)]
  transfers between devices with their start and end apart: 3 -> 3, of which waited for: 3 -> 3; matrix products, arithmetic and copies ran while one was open for 3% -> 1% of each run, Pallas kernels for 0% -> 0%
where the time goes in v1:
time: 2290 us
  waiting for transfers between devices  2180 us (95%)
  other arithmetic  44 us (2%)
  local copies, waits for them, and re-layouts  35 us (2%)
    all_gather x1, waiting for transfers between devices, local(): lax.all_gather(row_partials.astype(jnp.bfloat16), 'row')  2020 us
    reduce_scatter x1, waiting for transfers between devices, local(): lax.psum_scatter(column_term.astype(jnp.bfloat16), 'col', scatter_dimensi...  82.9 us
    all_gather x1, waiting for transfers between devices, local(): lax.all_gather(panel_local, 'col', axis=2, tiled=True)  73.9 us
  transfers between devices with their start and end apart: 3, of which 3 were waited for; matrix products, arithmetic and copies ran while one was open for 1% of the time, Pallas kernels for 0%

profile of v1, /device:TPU:1, one launch (start us, length us, event | category | flops | bytes accessed | tf_op | source)
XLA Modules:
  0.0 2287.9 jit_solution(5033939473639731193)
XLA Ops:
  6.5 0.0 copy-start
  6.5 0.0 all-gather.4.cloned.1.call-start
  6.5 1.0 slice.16
  7.6 0.1 copy.22
  7.7 0.9 slice.15
  8.7 0.1 copy.21
  8.8 0.8 pad_maximum_fusion
  9.6 0.0 all-gather.4.cloned.1.call-update
  9.6 0.0 all-gather.6.cloned.1.call-start
  9.7 73.9 %all-gather.4.cloned.1.call-done = bf16[2,768,2048]{1,2,0:T(8,128)(2,1)} async-done(((bf16[2,768,128]{1,2,0:T(8,128)(2,1)}), bf16[2,768,2048]{1,2,0:T(8,128)(2,1)}) %all-gather.4.cloned.1.call-update) | async-done | bytes 6291472 | tf_op jit(solution)/shard_map/all_gather | solution.py:17
  83.6 0.0 copy-done
  83.6 9.7 convert_bitcast_fusion
  93.3 8.7 copy.16
  102.0 0.0 all-gather.6.cloned.1.call-update
  102.0 0.2 reduce-scatter.2.cloned.1.call-start
  102.2 0.7 constant_dynamic-slice_fusion
  103.0 0.1 slice.17
  103.1 0.5 broadcast_in_dim.2
  103.5 5.6 copy.25
  109.1 6.8 copy.18
  115.9 2020.0 %all-gather.6.cloned.1.call-done = bf16[32,768,2048]{2,1,0:T(8,128)(2,1)} async-done(((bf16[2,768,2048]{2,1,0:T(8,128)(2,1)}), bf16[32,768,2048]{2,1,0:T(8,128)(2,1)}) %all-gather.6.cloned.1.call-update) | async-done | bytes 100663312 | tf_op jit(solution)/shard_map/all_gather | solution.py:28
  2135.9 34.7 %reduce_sum.12 = bf16[2,768,2048]{2,1,0:T(8,128)(2,1)} reduce(bf16[16,2,768,2048]{3,2,1,0:T(8,128)(2,1)} %bitcast.4, bf16[]{:T(256)} %constant.5.clone.1), dimensions={0}, to_apply=%region_0.0 | reduce | flops 47185920 | bytes 106954752 | tf_op jit(solution)/shard_map/reduce_sum | solution.py:28
  2170.6 8.6 copy.20
  2179.3 0.0 copy-start.3
  2179.3 8.5 multiply_convert_fusion
  2187.8 0.0 copy-done.3
  2187.8 0.0 copy-start.2
  2187.8 0.0 copy-start.4
  2187.8 4.7 fusion
  2192.5 0.0 copy-done.2
  2192.5 0.0 copy-done.4
  2192.5 0.0 copy-start.1
  2192.5 4.1 fusion.1
  2196.6 0.0 reduce-scatter.2.cloned.1.call-update
  2196.6 82.9 %reduce-scatter.2.cloned.1.call-done = bf16[768,128]{0,1:T(8,128)(2,1)} async-done(((bf16[768,2048]{0,1:T(8,128)(2,1)}), bf16[768,128]{0,1:T(8,128)(2,1)}) %reduce-scatter.2.cloned.1.call-update) | async-done | bytes 196624 | tf_op jit(solution)/shard_map/reduce_scatter | solution.py:36
  2279.6 1.7 copy.19
  2281.3 0.0 copy-done.1
  (1 shorter events, 0.0 us)
Async XLA Ops:
  6.5 77.0 %copy-start = (bf16[768,768]{1,0:T(8,128)(2,1)S(1)}, bf16[768,768]{1,0:T(8,128)(2,1)}, u32[]{:S(2)}) copy-start(bf16[768,768]{1,0:T(8,128)(2,1)} %param.5) | copy-start | bytes 3538948
  6.5 77.0 %all-gather.4.cloned.1.call-start = ((), (), s32[]{:S(2)}) async-start(), calls=%async_computation.1 | async-start | bytes 6684672 | tf_op jit(solution)/shard_map/all_gather | solution.py:17
  9.6 2126.3 %all-gather.6.cloned.1.call-start = ((), (), s32[]{:S(2)}) async-start(), calls=%async_computation.3 | async-start | bytes 106954752 | tf_op jit(solution)/shard_map/all_gather | solution.py:28
  102.0 2177.6 %reduce-scatter.2.cloned.1.call-start = ((), (), s32[]{:S(2)}) async-start(), calls=%async_computation.2 | async-start | bytes 3342336 | tf_op jit(solution)/shard_map/reduce_scatter | solution.py:36
  2179.3 8.5 copy-start.3
  2187.8 4.8 copy-start.2
  2187.8 4.8 copy-start.4
  2192.5 88.8 %copy-start.1 = (bf16[768,768]{1,0:T(8,128)(2,1)S(1)}, bf16[768,768]{1,0:T(8,128)(2,1)}, u32[]{:S(2)}) copy-start(bf16[768,768]{1,0:T(8,128)(2,1)} %param.5) | copy-start | bytes 3538948
Sparse Core Ops, SparseCore 0:
  10.2 73.3 all-gather.3
  102.1 2033.7 all-gather.5
  2196.8 82.7 reduce-scatter.1
